TPU v7x, 32 devices: a whole 2x2x4 slice. The times are simulated.
32 devices in a mesh: dom: 8 (over z, y), grp: 4 (over x, core).
Axes of the slice: x: 2, y: 2, z: 4, core: 2. Of those that a mesh axis runs over, the one named last changes fastest.
Arguments:
- nodes: bfloat16 [4, 4096, 128], P('grp', 'dom'), may hold values from -6 to 6
- edges: bfloat16 [4, 32, 128, 128], P('grp', 'dom'), may hold values from -6 to 6
- senders: int32 [4, 32, 128], P('grp', 'dom'), may hold values from 0 to 767
- receivers: int32 [4, 32, 128], P('grp', 'dom'), may hold values from 0 to 511
- block_count: int32 [4, 8], P('grp', 'dom'), may hold values from 1 to 4
- send_rows: int32 [4, 8, 2, 128], P('grp', 'dom'), may hold values from 0 to 511
- node_cot: bfloat16 [4, 4096, 128], P('grp', 'dom'), may hold values from -6 to 6
- edge_cot: bfloat16 [4, 32, 128, 128], P('grp', 'dom'), may hold values from -6 to 6
- edge_w1: bfloat16 [384, 128], replicated, may hold values from -0.3125 to 0.3125
- edge_b1: float32 [128], replicated, may hold values from -3 to 3
- edge_w2: bfloat16 [128, 128], replicated, may hold values from -0.5 to 0.5
- edge_b2: float32 [128], replicated, may hold values from -3 to 3
- edge_gain: float32 [128], replicated, may hold values from 0.5 to 1.5
- edge_shift: float32 [128], replicated, may hold values from -3 to 3
- node_w1: bfloat16 [256, 128], replicated, may hold values from -0.375 to 0.375
- node_b1: float32 [128], replicated, may hold values from -3 to 3
- node_w2: bfloat16 [128, 128], replicated, may hold values from -0.5 to 0.5
- node_b2: float32 [128], replicated, may hold values from -3 to 3
- node_gain: float32 [128], replicated, may hold values from 0.5 to 1.5
- node_shift: float32 [128], replicated, may hold values from -3 to 3
Outputs:
- node_out: bfloat16 [4, 4096, 128], P('grp', 'dom')
- edge_out: bfloat16 [4, 32, 128, 128], P('grp', 'dom')
- grad_node: bfloat16 [4, 4096, 128], P('grp', 'dom')
- grad_edge: bfloat16 [4, 32, 128, 128], P('grp', 'dom')
- weight_grads: float32 [115712], replicated
Inputs may be any that keep to these rules, and one draw needn't show every extreme that they name: `senders`: rows below 512 are the device's own nodes; row 512 + k holds the k-th row sent by the lower neighbouring partition, row 640 + k the k-th row sent by the upper one. `receivers`: receivers are own nodes of the device that holds the edge. `block_count`: A device's live blocks are its first ones; the rest are padding. send_rows[g, d, 0, :] are own rows of device d sent to device d - 1 of group g, send_rows[g, d, 1, :] those sent to device d + 1; they may repeat; lists toward no device are unused.
All inputs are finite; a program needn't handle non-finite values.
Results may differ from a plain program's by a relative error of at most 0.0054.
Values may be sent and summed in bfloat16 or wider, within the bound.
A program may use at most 64 MiB of HBM per device.

v0:
```python
import math

import jax
import jax.numpy as jnp
from jax import lax
from jax.sharding import PartitionSpec as P

EPSILON = 1e-05


def extended(value, sides, width):
    for axis, dim in sides:
        size, length = (lax.axis_size(axis), value.shape[dim])
        up = [(i, (i + 1) % size) for i in range(size - 1)]
        down = [(j, i) for i, j in up]
        last = lax.slice_in_dim(value, length - width, length, axis=dim)
        leading = lax.slice_in_dim(value, 0, width, axis=dim)
        before = lax.ppermute(last, axis, up)
        after = lax.ppermute(leading, axis, down)
        value = jnp.concatenate([before, value, after], axis=dim)
    return value


def norm_forward(pre_norm, norm_gain, norm_shift):
    average = jnp.mean(pre_norm, axis=-1, keepdims=True)
    centred = pre_norm - average
    variance = jnp.mean(centred * centred, axis=-1, keepdims=True)
    inverse = lax.rsqrt(variance + EPSILON)
    normed = centred * inverse
    return (normed * norm_gain + norm_shift, normed, inverse)


def norm_backward(grad_out, normed, inverse, norm_gain):
    scaled = grad_out * norm_gain
    return inverse * (
        scaled
        - jnp.mean(scaled, axis=-1, keepdims=True)
        - normed * jnp.mean(scaled * normed, axis=-1, keepdims=True)
    )


def silu_slope(pre_act):
    sigmoid = jax.nn.sigmoid(pre_act)
    return sigmoid * (1.0 + pre_act * (1.0 - sigmoid))


def row_product(left, right):
    return lax.dot_general(
        left, right, (((0,), (0,)), ((), ())), preferred_element_type=jnp.float32
    )


def mlp_forward(inputs, weights):
    w_first, b_first, w_second, b_second, norm_gain, norm_shift = weights
    first_pre = jnp.dot(inputs, w_first, preferred_element_type=jnp.float32) + b_first
    hidden = jax.nn.silu(first_pre).astype(jnp.bfloat16)
    second_pre = jnp.dot(hidden, w_second, preferred_element_type=jnp.float32) + b_second
    output, normed, inverse = norm_forward(second_pre, norm_gain, norm_shift)
    return (output, (first_pre, hidden, normed, inverse))


def mlp_backward(inputs, saved, grad_out, weights):
    w_first, b_first, w_second, b_second, norm_gain, norm_shift = weights
    first_pre, hidden, normed, inverse = saved
    grad_second = norm_backward(grad_out, normed, inverse, norm_gain)
    second_low = grad_second.astype(jnp.bfloat16)
    grad_hidden = jnp.dot(second_low, w_second.T, preferred_element_type=jnp.float32)
    grad_first = grad_hidden * silu_slope(first_pre)
    first_low = grad_first.astype(jnp.bfloat16)
    grad_inputs = jnp.dot(first_low, w_first.T, preferred_element_type=jnp.float32)
    grads = (
        row_product(inputs, first_low),
        jnp.sum(grad_first, axis=0),
        row_product(hidden, second_low),
        jnp.sum(grad_second, axis=0),
        jnp.sum(grad_out * normed, axis=0),
        jnp.sum(grad_out, axis=0),
    )
    return (grad_inputs, grads)


def shards(
    nodes,
    edges,
    senders,
    receivers,
    block_count,
    send_rows,
    node_cot,
    edge_cot,
    edge_w1,
    edge_b1,
    edge_w2,
    edge_b2,
    edge_gain,
    edge_shift,
    node_w1,
    node_b1,
    node_w2,
    node_b2,
    node_gain,
    node_shift,
):
    edge_weights = (edge_w1, edge_b1, edge_w2, edge_b2, edge_gain, edge_shift)
    node_weights = (node_w1, node_b1, node_w2, node_b2, node_gain, node_shift)
    own_nodes = nodes[0]
    node_rows, width = own_nodes.shape
    block_total = senders.shape[1]
    block_rows = senders.shape[2]
    edge_rows = block_total * block_rows
    flat_edges = edges[0].reshape(edge_rows, width)
    flat_send = senders[0].reshape(edge_rows)
    flat_recv = receivers[0].reshape(edge_rows)
    flat_cot = edge_cot[0].reshape(edge_rows, width)
    live_blocks = block_count[0, 0]
    row_lists = send_rows[0, 0]
    slot_count = row_lists.shape[1]
    outgoing = own_nodes[row_lists.reshape(-1)].reshape(2, slot_count, width)
    padded = extended(outgoing, (("dom", 0),), 1)
    from_lower, from_upper = (padded[0], padded[3])
    node_table = jnp.concatenate([own_nodes, from_lower, from_upper], axis=0)
    group_blocks = 4
    span = group_blocks * block_rows
    step_total = (live_blocks + group_blocks - 1) // group_blocks

    def edge_indices(offset):
        positions = offset + jnp.arange(span, dtype=jnp.int32)
        live_mask = (positions // block_rows < live_blocks).astype(jnp.float32)[:, None]
        return (flat_send, flat_recv, live_mask)

    def edge_inputs(send_part, recv_part):
        return jnp.concatenate([flat_edges, node_table[send_part], own_nodes[recv_part]], axis=1)

    stores = ()

    def forward_step(step_index, state_tuple):
        aggregate, edge_out, kept = state_tuple
        offset = step_index * span
        send_part, recv_part, live_mask = edge_indices(offset)
        inputs = edge_inputs(send_part, recv_part)
        message, saved = mlp_forward(inputs, edge_weights)
        live_message = message * live_mask
        aggregate = aggregate.at[recv_part].add(live_message)
        updated = (inputs[:, :width].astype(jnp.float32) + live_message).astype(jnp.bfloat16)
        edge_out = updated
        kept = tuple(
            (
                lax.dynamic_update_slice_in_dim(buffer, piece, offset, 0)
                for buffer, piece in zip(kept, (inputs,) + saved)
            )
        )
        return (aggregate, edge_out, kept)

    aggregate, edge_out, kept = lax.fori_loop(
        0,
        step_total,
        forward_step,
        (jnp.zeros((node_rows, width), jnp.float32), flat_edges, stores),
    )
    node_inputs = jnp.concatenate([own_nodes, aggregate.astype(jnp.bfloat16)], axis=1)
    update, node_saved = mlp_forward(node_inputs, node_weights)
    node_out = (own_nodes.astype(jnp.float32) + update).astype(jnp.bfloat16)
    node_grad = node_cot[0].astype(jnp.float32)
    grad_node_inputs, node_grads = mlp_backward(node_inputs, node_saved, node_grad, node_weights)
    grad_aggregate = grad_node_inputs[:, width:]

    def backward_step(step_index, state_tuple):
        table_grad, grad_edge, totals = state_tuple
        offset = step_index * span
        send_part, recv_part, live_mask = edge_indices(offset)
        inputs = edge_inputs(send_part, recv_part)
        unused_output, saved = mlp_forward(inputs, edge_weights)
        cot_part = flat_cot.astype(jnp.float32)
        grad_message = live_mask * (cot_part + grad_aggregate[recv_part])
        grad_inputs, step_grads = mlp_backward(inputs, saved, grad_message, edge_weights)
        new_grad = (cot_part + grad_inputs[:, :width]).astype(jnp.bfloat16)
        grad_edge = new_grad
        table_grad = table_grad.at[send_part].add(grad_inputs[:, width : 2 * width])
        table_grad = table_grad.at[recv_part].add(grad_inputs[:, 2 * width :])
        totals = tuple((total + piece for total, piece in zip(totals, step_grads)))
        return (table_grad, grad_edge, totals)

    zero_grads = tuple((jnp.zeros(piece.shape, jnp.float32) for piece in edge_weights))
    table_grad, grad_edge, edge_grads = lax.fori_loop(
        0,
        step_total,
        backward_step,
        (jnp.zeros((node_table.shape[0], width), jnp.float32), flat_cot, zero_grads),
    )
    halo_grad = table_grad[node_rows:].reshape(2, slot_count, width)
    padded_grad = extended(halo_grad.astype(jnp.bfloat16), (("dom", 0),), 1).astype(halo_grad.dtype)
    back_lower, back_upper = (padded_grad[0], padded_grad[3])
    returned = jnp.concatenate([back_lower, back_upper], axis=0)
    local_grad = node_grad + grad_node_inputs[:, :width] + table_grad[:node_rows]
    local_grad = local_grad.at[row_lists.reshape(-1)].add(returned)
    grad_node = local_grad.astype(jnp.bfloat16)
    flat_grads = jnp.concatenate([piece.reshape(-1) for piece in edge_grads + node_grads])
    summed = lax.psum(flat_grads, ("dom", "grp"))
    scale = 1.0 / math.sqrt(lax.axis_size("dom") * lax.axis_size("grp") * edge_rows)
    weight_grads = summed * scale
    return (
        node_out[None],
        edge_out.reshape(1, block_total, block_rows, width),
        grad_node[None],
        grad_edge.reshape(1, block_total, block_rows, width),
        weight_grads,
    )


def solution(mesh):
    return jax.shard_map(
        shards,
        mesh=mesh,
        in_specs=(
            P("grp", "dom", None),
            P("grp", "dom", None, None),
            P("grp", "dom", None),
            P("grp", "dom", None),
            P("grp", "dom"),
            P("grp", "dom", None, None),
            P("grp", "dom", None),
            P("grp", "dom", None, None),
            P(),
            P(),
            P(),
            P(),
            P(),
            P(),
            P(),
            P(),
            P(),
            P(),
            P(),
            P(),
        ),
        out_specs=(
            P("grp", "dom", None),
            P("grp", "dom", None, None),
            P("grp", "dom", None),
            P("grp", "dom", None, None),
            P(),
        ),
        check_vma=False,
    )
```

profile of v0, /device:TPU:0, one launch (start us, length us, event | category | flops | bytes accessed | tf_op | source)
XLA Modules:
  0.0 210.2 jit_solution(15320110725477557572)
XLA Ops:
  7.2 0.7 copy-done.20
  7.9 1.6 gather_fusion.1
  9.7 1.3 collective-permute-start.1
  11.1 5.7 %collective-permute-start = (bf16[1,128,128]{1,2,0:T(8,128)(2,1)S(1)}, bf16[1,128,128]{1,2,0:T(8,128)(2,1)S(1)}, u32[]{:S(2)}, u32[]{:S(2)}) collective-permute-start(bf16[1,128,128]{1,2,0:T(8,128)(2,1)S(1)} %bitcast.159), channel_id=1, source_target_pairs={{0,4},{4,8},{8,12},{12,16},{16,20},{20,24},{24,28},{1,5},{5,9},{9,... | collective-permute-start | bytes 98312 | tf_op jit(solution)/shard_map/ppermute | solution.py:18
  16.8 0.6 copy-done.13
  17.6 0.7 convert_reduce_fusion
  19.2 1.3 gather_fusion.3
  20.6 0.7 copy.88
  21.6 0.7 copy.79
  22.5 1.3 gather_fusion.2
  24.7 0.6 copy-done.9
  25.3 5.3 %while.42 = (s32[]{:T(128)}, f32[512,128]{1,0:T(8,128)S(1)}, bf16[512,128]{1,0:T(8,128)(2,1)}, s32[]{:T(128)}, s32[512]{0:T(512)S(1)}, /*index=5*/f32[128]{0:T(1...) while((s32[]{:T(128)}, f32[512,128]{1,0:T(8,128)S(1)}, ...), condition=%wide.region_4.5_spmd, body=%wide.region_2.4_spmd.sunk | while | flops 1060867 | bytes 1078433 | solution.py:154
  25.3 0.7 fusion.116
  26.0 0.9 add_convert_fusion.3
  26.9 3.7 %scatter_custom_fusion.15 = f32[512,128]{1,0:T(8,128)S(1)} fusion(f32[512,128]{1,0:T(8,128)S(1)} %get-tuple-element.1141, s32[512]{0:T(512)S(1)} %bitcast.155, f32[512,128]{1,0:T(8,128)S(1)} %get-tuple-element.1161, f32[512]{0:T(512)S(1)} %fusion.116, f32[128]{0:T(128)S(1)} %get-tuple-element.1165, f32[128]{0:T(128)S(1)} %get-tuple-element.1164, ...), kind=kCustom, calls=%fused_computation.11.clone.1 | custom fusion | flops 458752 | bytes 531968 | tf_op jit(solution)/shard_map/while/body/scatter-add | solution.py:143
  32.3 0.6 copy-done.18
  33.1 0.9 convolution_bitcast_fusion.1
  34.0 0.8 fusion.78
  34.9 0.9 convolution_bitcast_fusion
  36.0 0.7 fusion.73
  36.7 1.0 gather_fusion.4
  38.4 0.6 broadcast.465.clone.1
  40.1 17.7 %while.43 = (s32[]{:T(128)}, f32[768,128]{1,0:T(8,128)S(1)}, bf16[512,128]{0,1:T(8,128)(2,1)}, f32[384,128]{1,0:T(8,128)S(1)}, f32[128]{0:T(128)}, /*index=5*/f3...) while((s32[]{:T(128)}, f32[768,128]{1,0:T(8,128)S(1)}, ...), condition=%wide.region_20.21_spmd, body=%wide.region_9.20_spmd.sunk | while | flops 204813824 | bytes 10293525 | solution.py:184
  40.3 0.7 fusion.130
  41.0 1.3 gather_fusion
  43.4 1.1 add.621
  44.5 1.3 add.622
  45.8 1.1 add.623
  47.2 1.0 fusion.132
  48.5 1.1 add.620
  50.1 0.7 fusion.134
  50.8 3.5 %scatter_custom_fusion.18 = f32[768,128]{1,0:T(8,128)S(1)} fusion(f32[768,128]{1,0:T(8,128)S(1)} %get-tuple-element.1196, s32[512]{0:T(512)S(1)} %bitcast.147, f32[512,384]{1,0:T(8,128)S(1)} %fusion.133), kind=kCustom, calls=%fused_computation.43.clone.1 | custom fusion | flops 65536 | bytes 655360 | tf_op jit(solution)/shard_map/while/body/scatter-add | solution.py:178
  54.3 3.5 %scatter_custom_fusion.19 = f32[768,128]{1,0:T(8,128)S(1)} fusion(f32[768,128]{1,0:T(8,128)S(1)} %scatter_custom_fusion.18, s32[512]{0:T(512)S(1)} %bitcast.154, f32[512,384]{1,0:T(8,128)S(1)} %fusion.133), kind=kCustom, calls=%fused_computation.41.clone.1 | custom fusion | flops 65536 | bytes 655360 | tf_op jit(solution)/shard_map/while/body/scatter-add | solution.py:179
  58.0 0.8 copy-done.4
  59.0 4.8 %collective-permute-start.2 = (bf16[1,128,128]{2,1,0:T(8,128)(2,1)S(1)}, bf16[1,128,128]{2,1,0:T(8,128)(2,1)S(1)}, u32[]{:S(2)}, u32[]{:S(2)}) collective-permute-start(bf16[1,128,128]{2,1,0:T(8,128)(2,1)S(1)} %get-tuple-element.858), channel_id=1, source_target_pairs={{0,4},{4,8},{8,12},{12,16},{16,20},{20,24},{24,28},{1,5},{5,9},{9,... | collective-permute-start | bytes 98312 | tf_op jit(solution)/shard_map/ppermute | solution.py:18
  63.8 1.3 collective-permute-start.3
  65.2 0.6 constant_dynamic-update-slice_fusion.12
  65.8 0.6 constant_dynamic-update-slice_fusion.11
  66.4 0.7 constant_dynamic-update-slice_fusion.10
  67.1 0.6 constant_dynamic-update-slice_fusion.9
  68.6 0.6 copy-done.19
  70.4 0.8 copy.61
  71.1 0.8 copy.62
  72.1 0.8 slice-done
  72.9 2.1 scatter_custom_fusion.3
  75.0 0.7 convert_bitcast_fusion.1
  75.6 125.9 %all-reduce.2.cloned.1.call-done = f32[115712]{0:T(1024)} async-done(((f32[115712]{0:T(1024)}), f32[115712]{0:T(1024)}) %all-reduce.2.cloned.1.call-update) | async-done | bytes 462864 | tf_op jit(solution)/shard_map/psum | solution.py:198
  201.5 1.8 broadcast_multiply_fusion.4
  (130 shorter events, 10.3 us)
Async XLA Ops:
  7.2 23.5 %copy-start = (bf16[256,128]{1,0:T(8,128)(2,1)S(1)}, bf16[256,128]{1,0:T(8,128)(2,1)}, u32[]{:S(2)}) copy-start(bf16[256,128]{1,0:T(8,128)(2,1)} %param.38) | copy-start | bytes 196612
  7.2 0.7 copy-start.20
  7.2 194.4 %all-reduce.2.cloned.1.call-start = ((), (), s32[]{:S(2)}) async-start(), calls=%async_computation | async-start | bytes 925696 | tf_op jit(solution)/shard_map/psum | solution.py:198
  9.6 7.9 %copy-start.10 = (bf16[1,512,128]{2,1,0:T(8,128)(2,1)S(1)}, bf16[1,512,128]{2,1,0:T(8,128)(2,1)}, u32[]{:S(2)}) copy-start(bf16[1,512,128]{2,1,0:T(8,128)(2,1)} %param.30) | copy-start | bytes 393220
  9.7 12.6 %collective-permute-start.1 = (bf16[1,128,128]{1,2,0:T(8,128)(2,1)S(1)}, bf16[1,128,128]{1,2,0:T(8,128)(2,1)S(1)}, u32[]{:S(2)}, u32[]{:S(2)}) collective-permute-start(bf16[1,128,128]{1,2,0:T(8,128)(2,1)S(1)} %bitcast.158), channel_id=1, source_target_pairs={{4,0},{8,4},{12,8},{16,12},{20,16},{24,20},{28,24},{5,1},{9,5},{13... | collective-permute-start | bytes 98312 | tf_op jit(solution)/shard_map/ppermute | solution.py:19
  11.1 5.7 %copy-start.8 = (s32[1,4,128]{2,1,0:T(4,128)S(1)}, s32[1,4,128]{2,1,0:T(4,128)}, u32[]{:S(2)}) copy-start(s32[1,4,128]{2,1,0:T(4,128)} %param.27) | copy-start | bytes 6148
  11.1 11.1 %collective-permute-start = (bf16[1,128,128]{1,2,0:T(8,128)(2,1)S(1)}, bf16[1,128,128]{1,2,0:T(8,128)(2,1)S(1)}, u32[]{:S(2)}, u32[]{:S(2)}) collective-permute-start(bf16[1,128,128]{1,2,0:T(8,128)(2,1)S(1)} %bitcast.159), channel_id=1, source_target_pairs={{0,4},{4,8},{8,12},{12,16},{16,20},{20,24},{24,28},{1,5},{5,9},{9,... | collective-permute-start | bytes 98312 | tf_op jit(solution)/shard_map/ppermute | solution.py:18
  16.8 0.7 copy-start.13
  17.6 1.4 copy-start.1
  19.1 1.4 copy-start.11
  20.6 1.0 copy-start.2
  22.4 1.4 copy-start.3
  22.4 1.4 copy-start.15
  22.5 1.4 copy-start.17
  22.5 1.4 copy-start.25
  24.6 0.7 copy-start.9
  24.6 0.7 copy-start.16
  30.6 0.7 copy-start.23
  31.2 0.8 copy-start.24
  31.2 0.8 copy-start.27
  32.3 0.7 copy-start.18
  54.3 3.5 %copy-start.26 = (bf16[128,128]{1,0:T(8,128)(2,1)S(1)}, bf16[128,128]{1,0:T(8,128)(2,1)}, u32[]{:S(2)}) copy-start(bf16[128,128]{1,0:T(8,128)(2,1)} %get-tuple-element.1286) | copy-start | bytes 98308 | tf_op jit(solution)/shard_map/while
  57.8 12.1 %copy-start.6 = (bf16[768,128]{1,0:T(8,128)(2,1)}, bf16[768,128]{1,0:T(8,128)(2,1)S(1)}, u32[]{:S(2)}) copy-start(bf16[768,128]{1,0:T(8,128)(2,1)S(1)} %convert.3) | copy-start | bytes 589828
  57.8 1.0 copy-start.4
  59.0 13.1 %collective-permute-start.2 = (bf16[1,128,128]{2,1,0:T(8,128)(2,1)S(1)}, bf16[1,128,128]{2,1,0:T(8,128)(2,1)S(1)}, u32[]{:S(2)}, u32[]{:S(2)}) collective-permute-start(bf16[1,128,128]{2,1,0:T(8,128)(2,1)S(1)} %get-tuple-element.858), channel_id=1, source_target_pairs={{0,4},{4,8},{8,12},{12,16},{16,20},{20,24},{24,28},{1,5},{5,9},{9,... | collective-permute-start | bytes 98312 | tf_op jit(solution)/shard_map/ppermute | solution.py:18
  63.8 8.3 %collective-permute-start.3 = (bf16[1,128,128]{2,1,0:T(8,128)(2,1)S(1)}, bf16[1,128,128]{2,1,0:T(8,128)(2,1)S(1)}, u32[]{:S(2)}, u32[]{:S(2)}) collective-permute-start(bf16[1,128,128]{2,1,0:T(8,128)(2,1)S(1)} %get-tuple-element.859), channel_id=1, source_target_pairs={{4,0},{8,4},{12,8},{16,12},{20,16},{24,20},{28,24},{5,1},{9,5},{13... | collective-permute-start | bytes 98312 | tf_op jit(solution)/shard_map/ppermute | solution.py:19
  65.1 2.6 %copy-start.12 = (f32[32768]{0:T(1024)S(1)}, f32[32768]{0:T(1024)}, u32[]{:S(2)}) copy-start(f32[32768]{0:T(1024)} %convolution_bitcast_fusion) | copy-start | bytes 393220
  67.7 0.8 copy-start.14
  67.8 0.6 copy-start.28
  68.6 0.7 copy-start.19
  68.6 0.7 copy-start.21
  69.2 0.7 copy-start.22
  69.5 0.9 copy-start.7
  69.9 2.1 %copy-start.5 = (f32[115712]{0:T(1024)}, f32[115712]{0:T(1024)S(1)}, u32[]{:S(2)}) copy-start(f32[115712]{0:T(1024)S(1)} %constant_dynamic-update-slice_fusion.3) | copy-start | bytes 1388548
  72.0 0.8 slice-start
Sparse Core Ops, SparseCore 0:
  72.2 129.3 all-reduce.1
where the time goes:
time: 211 us; the launch traced here: 210 us
  waiting for transfers between devices  126 us (60%)
  local copies, waits for them, and re-layouts  24.7 us (12%)
  other arithmetic  24.5 us (12%)
  between operations  15.3 us (7%)
  starting transfers between devices  13.1 us (6%)
  matrix products  6.24 us (3%)
    psum x1, waiting for transfers between devices, shards(): summed = lax.psum(flat_grads, ('dom', 'grp'))  126 us
    unnamed x75, local copies, waits for them, and re-layouts  12.4 us
    ppermute x2, starting transfers between devices, extended(): before = lax.ppermute(last, axis, up)  10.5 us
    add x4, other arithmetic, backward_step(): totals = tuple((total + piece for total, piece in zip(totals, step_grads)))  4.61 us
  transfers between devices with their start and end apart: 5, of which 1 were waited for; matrix products, arithmetic and copies ran while one was open for 5% of the time, Pallas kernels for 0%

commit v1 on v0

v1 whole, which is shorter than its diff:
```python
import functools
import math

import jax
import jax.numpy as jnp
from jax import lax
from jax.experimental import pallas as pl
from jax.experimental.pallas import tpu as pltpu
from jax.sharding import PartitionSpec as P

EPSILON = 1e-05
BF = jnp.bfloat16
F32 = jnp.float32


def dot(a, b):
    return lax.dot_general(a, b, (((1,), (0,)), ((), ())), preferred_element_type=F32)


def dot_t(a, b):
    return lax.dot_general(a, b, (((1,), (1,)), ((), ())), preferred_element_type=F32)


def row_product(a, b):
    return lax.dot_general(a, b, (((0,), (0,)), ((), ())), preferred_element_type=F32)


def split(x):
    high = x.astype(BF)
    low = (x - high.astype(F32)).astype(BF)
    return high, low


def pair(x):
    return jnp.concatenate(split(x), axis=1)


def folded(x):
    half = x.shape[1] // 2
    return x[:, :half] + x[:, half:]


def norm_forward(pre_norm):
    average = jnp.mean(pre_norm, axis=-1, keepdims=True)
    centred = pre_norm - average
    variance = jnp.mean(centred * centred, axis=-1, keepdims=True)
    inverse = lax.rsqrt(variance + EPSILON)
    return centred * inverse, inverse


def norm_backward(grad_out, normed, inverse, gain):
    scaled = grad_out * gain
    return inverse * (
        scaled
        - jnp.mean(scaled, axis=-1, keepdims=True)
        - normed * jnp.mean(scaled * normed, axis=-1, keepdims=True)
    )


def slope_of(pre_act, sigmoid):
    return sigmoid * (1.0 + pre_act * (1.0 - sigmoid))


def column_sum(x):
    return jnp.sum(x, axis=0, keepdims=True)


def fill_rows(ref, ids_ref, count, width):
    for b in range(ids_ref.shape[0]):
        ids = jnp.broadcast_to(ids_ref[b : b + 1, :], (width, width)).T
        lane = lax.broadcasted_iota(jnp.int32, (width, width), 1)
        for c in range(count // width):
            ref[b * width : (b + 1) * width, c * width : (c + 1) * width] = jnp.where(
                ids == lane + c * width, 1.0, 0.0
            ).astype(BF)


def fill_columns(ref, ids_ref, count, width):
    for b in range(ids_ref.shape[0]):
        ids = ids_ref[b : b + 1, :]
        row = lax.broadcasted_iota(jnp.int32, (count, width), 0)
        ref[:, b * width : (b + 1) * width] = jnp.where(row == ids, 1.0, 0.0).astype(BF)


def kernel(
    sizes,
    count_ref, nodes_ref, edges_ref, send_ref, recv_ref, rows_ref, ncot_ref, ecot_ref,
    ew1, eb1, ew2, eb2, eg, es, nw1, nb1, nw2, nb2, ng, ns,
    node_out, edge_out, grad_node, grad_edge, weight_out,
    oh_s, oh_st, oh_r, oh_rt, oh_x, oh_xt,
    halo_out, halo_in, back_out, back_in,
    part_a, part_b, got_a, got_b, red_a, red_b, all_a, all_b,
    halo_send, halo_recv, back_send, back_recv,
    rs_send, rs_recv, ag_send, ag_recv,
):
    n_dom, n_grp, chunk, scale = sizes
    total = n_dom * n_grp
    d = lax.axis_index("dom")
    g = lax.axis_index("grp")
    rank = d * n_grp + g
    rows, width = nodes_ref.shape
    edge_rows = edges_ref.shape[0]
    slots = rows_ref.shape[1]
    lower = lax.rem(d + n_dom - 1, n_dom)
    upper = lax.rem(d + 1, n_dom)

    def target(k):
        t = lax.rem(rank + k, total)
        return t, {"dom": t // n_grp, "grp": lax.rem(t, n_grp)}

    barrier = pltpu.get_barrier_semaphore()

    def greet(k, carry):
        pl.semaphore_signal(
            barrier, inc=1, device_id=target(k)[1], device_id_type=pl.DeviceIdType.MESH
        )
        return carry

    lax.fori_loop(1, total, greet, 0)

    nodes = nodes_ref[...]
    fill_rows(oh_x, rows_ref, rows, width)
    halo_out[...] = dot(oh_x[...], nodes).astype(BF)

    pl.semaphore_wait(barrier, total - 1)

    def swap(out, into, send_sem, recv_sem):
        copies = []
        for side, neighbour in ((0, lower), (1, upper)):
            copy = pltpu.make_async_remote_copy(
                src_ref=out.at[pl.ds(side * slots, slots)],
                dst_ref=into.at[pl.ds((1 - side) * slots, slots)],
                send_sem=send_sem.at[side],
                recv_sem=recv_sem.at[1 - side],
                device_id={"dom": neighbour, "grp": g},
                device_id_type=pl.DeviceIdType.MESH,
            )
            copy.start()
            copies.append(copy)
        return copies

    halo_copies = swap(halo_out, halo_in, halo_send, halo_recv)

    fill_rows(oh_r, recv_ref, rows, width)
    fill_rows(oh_s, send_ref, rows + 2 * slots, width)
    fill_columns(oh_rt, recv_ref, rows, width)
    fill_columns(oh_st, send_ref, rows + 2 * slots, width)
    fill_columns(oh_xt, rows_ref, rows, width)

    live = (
        lax.broadcasted_iota(jnp.int32, (edge_rows, width), 0) < count_ref[0, 0] * width
    ).astype(F32)
    edges = edges_ref[...]
    at_recv = dot(oh_r[...], nodes).astype(BF)
    at_own = dot(oh_s[:, :rows], nodes)
    first = dot(edges, ew1[:width, :]) + dot(at_recv, ew1[2 * width :, :])

    for copy in halo_copies:
        copy.wait()
    from_lower = halo_in[:slots, :] * (d > 0).astype(BF)
    from_upper = halo_in[slots:, :] * (d < n_dom - 1).astype(BF)
    at_halo = dot(oh_s[:, rows : rows + slots], from_lower) + dot(
        oh_s[:, rows + slots :], from_upper
    )
    at_send = (at_own + at_halo).astype(BF)
    first = first + dot(at_send, ew1[width : 2 * width, :]) + eb1[...]
    sigmoid = lax.logistic(first)
    hidden = (first * sigmoid).astype(BF)
    slope = slope_of(first, sigmoid)
    second = dot(hidden, ew2[...]) + eb2[...]
    normed, inverse = norm_forward(second)
    message = (normed * eg[...] + es[...]) * live
    edge_out[...] = (edges.astype(F32) + message).astype(BF)
    aggregate = folded(dot(oh_rt[...], pair(message))).astype(BF)

    n_inputs = jnp.concatenate([nodes, aggregate], axis=1)
    n_first = dot(n_inputs, nw1[...]) + nb1[...]
    n_sigmoid = lax.logistic(n_first)
    n_hidden = (n_first * n_sigmoid).astype(BF)
    n_second = dot(n_hidden, nw2[...]) + nb2[...]
    n_normed, n_inverse = norm_forward(n_second)
    node_out[...] = (nodes.astype(F32) + (n_normed * ng[...] + ns[...])).astype(BF)

    n_cot = ncot_ref[...].astype(F32)
    n_g2 = norm_backward(n_cot, n_normed, n_inverse, ng[...])
    n_g2_low = n_g2.astype(BF)
    n_g1 = dot_t(n_g2_low, nw2[...]) * slope_of(n_first, n_sigmoid)
    n_g1_low = n_g1.astype(BF)
    n_dx = dot_t(n_g1_low, nw1[...])

    e_cot = ecot_ref[...].astype(F32)
    c = live * (e_cot + folded(dot(oh_r[...], pair(n_dx[:, width:]))))
    g2 = norm_backward(c, normed, inverse, eg[...])
    g2_low = g2.astype(BF)

    part_a[: 2 * width, :] = row_product(n_inputs, n_g1_low).astype(BF)
    part_a[2 * width : 3 * width, :] = row_product(n_hidden, n_g2_low).astype(BF)
    part_a[3 * width : 4 * width, :] = row_product(hidden, g2_low).astype(BF)
    if part_a.shape[0] > 4 * width:
        part_a[4 * width :, :] = jnp.zeros((part_a.shape[0] - 4 * width, width), BF)

    def scatter(part, got, which):
        def step(k, carry):
            t, device = target(k)
            pltpu.make_async_remote_copy(
                src_ref=part.at[pl.ds(pl.multiple_of(t * chunk, chunk), chunk)],
                dst_ref=got.at[pl.ds(pl.multiple_of(k * chunk, chunk), chunk)],
                send_sem=rs_send.at[which],
                recv_sem=rs_recv.at[which],
                device_id=device,
                device_id_type=pl.DeviceIdType.MESH,
            ).start()
            return carry

        lax.fori_loop(1, total, step, 0)

    def drain(ref, sem):
        span = ref.at[pl.ds(chunk, (total - 1) * chunk)]
        pltpu.make_async_copy(span, span, sem).wait()

    scatter(part_a, got_a, 0)

    g1 = dot_t(g2_low, ew2[...]) * slope
    g1_low = g1.astype(BF)
    at_table = dot(oh_st[...], g1_low)
    high, low = split(at_table[rows:, :])
    w_send = ew1[width : 2 * width, :]
    back_out[...] = (dot_t(high, w_send) + dot_t(low, w_send)).astype(BF)
    back_copies = swap(back_out, back_in, back_send, back_recv)

    part_b[:width, :] = row_product(edges, g1_low).astype(BF)
    part_b[width : 2 * width, :] = row_product(at_send, g1_low).astype(BF)
    part_b[2 * width : 3 * width, :] = row_product(at_recv, g1_low).astype(BF)
    small = jnp.concatenate(
        [
            column_sum(g1),
            column_sum(g2),
            column_sum(c * normed),
            column_sum(c),
            column_sum(n_g1),
            column_sum(n_g2),
            column_sum(n_cot * n_normed),
            column_sum(n_cot),
            jnp.zeros((part_b.shape[0] - 3 * width - 8, width), F32),
        ],
        axis=0,
    )
    part_b[3 * width :, :] = small.astype(BF)
    scatter(part_b, got_b, 1)

    grad_edge[...] = (e_cot + dot_t(g1_low, ew1[:width, :])).astype(BF)
    at_receiver = dot(oh_rt[...], g1_low)
    both = jnp.concatenate([at_table[:rows, :], at_receiver], axis=1)
    w_both = jnp.concatenate([w_send, ew1[2 * width :, :]], axis=1)
    high, low = split(both)
    local = n_cot + n_dx[:, :width] + dot_t(high, w_both) + dot_t(low, w_both)

    def reduce(part, got, red, whole, which):
        drain(got, rs_recv.at[which])
        mine = pl.ds(pl.multiple_of(rank * chunk, chunk), chunk)
        summed = part[mine, :].astype(F32)
        for k in range(1, total):
            summed = summed + got[k * chunk : (k + 1) * chunk, :].astype(F32)
        result = (summed * scale).astype(BF)
        red[...] = result
        whole[mine, :] = result

        def step(k, carry):
            pltpu.make_async_remote_copy(
                src_ref=red,
                dst_ref=whole.at[mine],
                send_sem=ag_send.at[which],
                recv_sem=ag_recv.at[which],
                device_id=target(k)[1],
                device_id_type=pl.DeviceIdType.MESH,
            ).start()
            return carry

        lax.fori_loop(1, total, step, 0)

    reduce(part_a, got_a, red_a, all_a, 0)

    for copy in back_copies:
        copy.wait()
    back_lower = back_in[:slots, :] * (d > 0).astype(BF)
    back_upper = back_in[slots:, :] * (d < n_dom - 1).astype(BF)
    returned = dot(oh_xt[:, :slots], back_lower) + dot(oh_xt[:, slots:], back_upper)
    grad_node[...] = (local + returned).astype(BF)

    reduce(part_b, got_b, red_b, all_b, 1)

    edge_size = 4 * width + 4
    drain(all_a, ag_recv.at[0])
    weight_out[edge_size : edge_size + 2 * width, :] = all_a[: 2 * width, :].astype(F32)
    at = edge_size + 2 * width + 1
    weight_out[at : at + width, :] = all_a[2 * width : 3 * width, :].astype(F32)
    at = 3 * width + 1
    weight_out[at : at + width, :] = all_a[3 * width : 4 * width, :].astype(F32)
    drain(all_b, ag_recv.at[1])
    weight_out[: 3 * width, :] = all_b[: 3 * width, :].astype(F32)
    small = all_b[3 * width : 3 * width + 16, :].astype(F32)
    weight_out[3 * width : 3 * width + 1, :] = small[0:1, :]
    weight_out[4 * width + 1 : 4 * width + 4, :] = small[1:4, :]
    weight_out[edge_size + 2 * width : edge_size + 2 * width + 1, :] = small[4:5, :]
    weight_out[edge_size + 3 * width + 1 : edge_size + 3 * width + 4, :] = small[5:8, :]

    drain(got_a, rs_send.at[0])
    drain(got_b, rs_send.at[1])
    drain(all_a, ag_send.at[0])
    drain(all_b, ag_send.at[1])


def shards(
    nodes, edges, senders, receivers, block_count, send_rows, node_cot, edge_cot,
    edge_w1, edge_b1, edge_w2, edge_b2, edge_gain, edge_shift,
    node_w1, node_b1, node_w2, node_b2, node_gain, node_shift,
):
    n_dom, n_grp = lax.axis_size("dom"), lax.axis_size("grp")
    total = n_dom * n_grp
    _, rows, width = nodes.shape
    _, blocks, block_rows, _ = edges.shape
    edge_rows = blocks * block_rows
    slots = send_rows.shape[3]
    chunk = -(-4 * width // (16 * total)) * 16
    padded = chunk * total
    scale = 1.0 / math.sqrt(total * edge_rows)
    vmem = pl.BlockSpec(memory_space=pltpu.VMEM)
    line = lambda v: v.reshape(1, -1)
    grads = 2 * (4 + width) * width + (3 + 2) * width * width
    sem = pltpu.SemaphoreType.DMA((2,))
    table = rows + 2 * slots
    node_out, edge_out, grad_node, grad_edge, weights = pl.pallas_call(
        functools.partial(kernel, (n_dom, n_grp, chunk, scale)),
        out_shape=(
            jax.ShapeDtypeStruct((rows, width), BF),
            jax.ShapeDtypeStruct((edge_rows, width), BF),
            jax.ShapeDtypeStruct((rows, width), BF),
            jax.ShapeDtypeStruct((edge_rows, width), BF),
            jax.ShapeDtypeStruct((grads // width, width), F32),
        ),
        in_specs=[pl.BlockSpec(memory_space=pltpu.SMEM)] + [vmem] * 19,
        out_specs=[vmem] * 5,
        scratch_shapes=[
            pltpu.VMEM((edge_rows, table), BF),
            pltpu.VMEM((table, edge_rows), BF),
            pltpu.VMEM((edge_rows, rows), BF),
            pltpu.VMEM((rows, edge_rows), BF),
            pltpu.VMEM((2 * slots, rows), BF),
            pltpu.VMEM((rows, 2 * slots), BF),
        ]
        + [pltpu.VMEM((2 * slots, width), BF)] * 4
        + [pltpu.VMEM((padded, width), BF)] * 4
        + [pltpu.VMEM((chunk, width), BF)] * 2
        + [pltpu.VMEM((padded, width), BF)] * 2
        + [sem] * 8,
        compiler_params=pltpu.CompilerParams(collective_id=0, has_side_effects=True),
    )(
        block_count,
        nodes[0],
        edges.reshape(edge_rows, width),
        senders[0],
        receivers[0],
        send_rows.reshape(2, slots),
        node_cot[0],
        edge_cot.reshape(edge_rows, width),
        edge_w1, line(edge_b1), edge_w2, line(edge_b2), line(edge_gain), line(edge_shift),
        node_w1, line(node_b1), node_w2, line(node_b2), line(node_gain), line(node_shift),
    )
    return (
        node_out[None],
        edge_out.reshape(edges.shape),
        grad_node[None],
        grad_edge.reshape(edges.shape),
        weights.reshape(-1),
    )


def solution(mesh):
    by_node = P("grp", "dom", None)
    by_edge = P("grp", "dom", None, None)
    return jax.shard_map(
        shards,
        mesh=mesh,
        in_specs=(
            by_node, by_edge, by_node, by_node, P("grp", "dom"), by_edge, by_node, by_edge,
        )
        + (P(),) * 12,
        out_specs=(by_node, by_edge, by_node, by_edge, P()),
        check_vma=False,
    )
```

time: 211 us -> 37.4 us (0.18)
  waiting for transfers between devices: 126 us -> 0 us
  Pallas kernels: 0 us -> 30.3 us
  other arithmetic: 24.5 us -> 0 us
  local copies, waits for them, and re-layouts: 24.7 us -> 5.61 us
  between operations: 15.3 us -> 1.31 us
  starting transfers between devices: 13.1 us -> 0 us
  matrix products: 6.24 us -> 0 us
    psum x1 -> x0, waiting for transfers between devices: 126 us -> none  [shards(): summed = lax.psum(flat_grads, ('dom', 'grp'))]
    pallas_call x0 -> x1, Pallas kernels: none -> 30.3 us  [shards(): pl.pallas_call(functools.partial(kernel, (n_dom, n_grp, chunk, scale)), o...]
    ppermute x4 -> x0, starting transfers between devices: 13.1 us -> none  [the longest x2 10.5 us: extended(): before = lax.ppermute(last, axis, up)]
    scatter-add x4 -> x0, other arithmetic: 12.7 us -> none  [the longest x1 3.67 us: forward_step(): aggregate = aggregate.at[recv_part].add(live_message)]
    unnamed x75 -> x11, local copies, waits for them, and re-layouts: 12.4 us -> 5.61 us
    gather x5 -> x0, local copies, waits for them, and re-layouts: 6.7 us -> none  [the longest x2 2.68 us: edge_inputs(): node_table[send_part]]
    dot_general x13 -> x0, matrix products: 6.24 us -> none  [the longest x4 2.4 us: row_product(): lax.dot_general(left, right, (((0,), (0,)), ((), ())), preferred_element_...]
    add x4 -> x0, other arithmetic: 4.61 us -> none  [backward_step(): totals = tuple((total + piece for total, piece in zip(totals, step_grads)))]
  transfers between devices with their start and end apart: 5 -> 0, of which waited for: 1 -> 0; matrix products, arithmetic and copies ran while one was open for 5% -> 0% of each run, Pallas kernels for 0% -> 0%
where the time goes in v1:
time: 37.4 us; the launch traced here: 37.2 us
  Pallas kernels  30.3 us (81%)
  local copies, waits for them, and re-layouts  5.61 us (15%)
  between operations  1.31 us (4%)
    pallas_call x1, Pallas kernels, shards(): pl.pallas_call(functools.partial(kernel, (n_dom, n_grp, chunk, scale)), o...  30.3 us
    unnamed x11, local copies, waits for them, and re-layouts  5.61 us

profile of v1, /device:TPU:0, one launch (start us, length us, event | category | flops | bytes accessed | tf_op | source)
XLA Modules:
  0.0 37.2 jit_solution(8008714494773475766)
XLA Ops:
  1.3 30.3 %shard_map.227 = (bf16[512,128]{1,0:T(8,128)(2,1)}, bf16[512,128]{1,0:T(8,128)(2,1)}, bf16[512,128]{1,0:T(8,128)(2,1)}, bf16[512,128]{1,0:T(8,128)(2,1)}, f32[904,128]{1,0:T(8,128)}) custom-call(s32[1,1]{1,0:T(1,128)S(6)} %copy.30.count_ref, bf16[512,128]{1,0:T(8,128)(2,1)} %bitcast.25, bf16[512,128]{1,0:T(8,128)(2,1)} %bitcast.26, s32[4,128]{1,0:T(4,128)} %bitcast.29, ...), custom_call_target="tpu_custom_call" | custom-call | tf_op jit(solution)/shard_map/pallas_call | solution.py:332
  31.6 0.0 copy-start.2
  31.6 0.0 copy-start
  31.6 1.6 %copy.31 = bf16[1,512,128]{2,1,0:T(8,128)(2,1)} copy(bf16[1,512,128]{2,1,0:T(8,128)(2,1)} %bitcast.24) | data formatting | bytes 262144
  33.3 1.6 %copy.32 = bf16[1,4,128,128]{3,2,1,0:T(8,128)(2,1)} copy(bf16[1,4,128,128]{3,2,1,0:T(8,128)(2,1)} %bitcast.23) | data formatting | bytes 262144
  34.8 0.0 copy-done.2
  34.8 0.0 copy-start.1
  34.8 0.7 %copy.33 = bf16[1,512,128]{2,1,0:T(8,128)(2,1)} copy(bf16[1,512,128]{2,1,0:T(8,128)(2,1)S(1)} %bitcast.22) | data formatting | bytes 262144
  35.5 0.3 copy-done.1
  35.8 0.7 %copy.34 = bf16[1,4,128,128]{3,2,1,0:T(8,128)(2,1)} copy(bf16[1,4,128,128]{3,2,1,0:T(8,128)(2,1)S(1)} %bitcast.21) | data formatting | bytes 262144
  36.4 0.0 copy-done
  36.4 0.8 %copy.35 = f32[115712]{0:T(1024)} copy(f32[115712]{0:T(1024)S(1)} %bitcast.20) | data formatting | bytes 925696
Async XLA Ops:
  31.6 3.2 %copy-start.2 = (bf16[512,128]{1,0:T(8,128)(2,1)S(1)}, bf16[512,128]{1,0:T(8,128)(2,1)}, u32[]{:S(2)}) copy-start(bf16[512,128]{1,0:T(8,128)(2,1)} %get-tuple-element.12) | copy-start | bytes 393220
  31.6 4.8 %copy-start = (f32[904,128]{1,0:T(8,128)S(1)}, f32[904,128]{1,0:T(8,128)}, u32[]{:S(2)}) copy-start(f32[904,128]{1,0:T(8,128)} %get-tuple-element.14) | copy-start | bytes 1388548
  34.8 1.0 %copy-start.1 = (bf16[512,128]{1,0:T(8,128)(2,1)S(1)}, bf16[512,128]{1,0:T(8,128)(2,1)}, u32[]{:S(2)}) copy-start(bf16[512,128]{1,0:T(8,128)(2,1)} %get-tuple-element.13) | copy-start | bytes 393220

commit v2 on v1

--- a/solution.py
+++ b/solution.py
@@ -88,7 +88,7 @@
     ew1, eb1, ew2, eb2, eg, es, nw1, nb1, nw2, nb2, ng, ns,
     node_out, edge_out, grad_node, grad_edge, weight_out,
     oh_s, oh_st, oh_r, oh_rt, oh_x, oh_xt,
-    halo_out, halo_in, back_out, back_in,
+    count_here, count_sem, part_first, part_send, halo_out, halo_in, back_out, back_in,
     part_a, part_b, got_a, got_b, red_a, red_b, all_a, all_b,
     halo_send, halo_recv, back_send, back_recv,
     rs_send, rs_recv, ag_send, ag_recv,
@@ -108,6 +108,8 @@
         t = lax.rem(rank + k, total)
         return t, {"dom": t // n_grp, "grp": lax.rem(t, n_grp)}
 
+    count_copy = pltpu.make_async_copy(count_ref, count_here, count_sem)
+    count_copy.start()
     barrier = pltpu.get_barrier_semaphore()
 
     def greet(k, carry):
@@ -122,11 +124,11 @@
     fill_rows(oh_x, rows_ref, rows, width)
     halo_out[...] = dot(oh_x[...], nodes).astype(BF)
 
-    pl.semaphore_wait(barrier, total - 1)
-
-    def swap(out, into, send_sem, recv_sem):
-        copies = []
-        for side, neighbour in ((0, lower), (1, upper)):
+    has_lower = d > 0
+    has_upper = d < n_dom - 1
+
+    def swap(out, into, send_sem, recv_sem, act):
+        for side, neighbour, there in ((0, lower, has_lower), (1, upper, has_upper)):
             copy = pltpu.make_async_remote_copy(
                 src_ref=out.at[pl.ds(side * slots, slots)],
                 dst_ref=into.at[pl.ds((1 - side) * slots, slots)],
@@ -135,11 +137,31 @@
                 device_id={"dom": neighbour, "grp": g},
                 device_id_type=pl.DeviceIdType.MESH,
             )
-            copy.start()
-            copies.append(copy)
-        return copies
-
-    halo_copies = swap(halo_out, halo_in, halo_send, halo_recv)
+            back = pltpu.make_async_remote_copy(
+                src_ref=out.at[pl.ds((1 - side) * slots, slots)],
+                dst_ref=into.at[pl.ds(side * slots, slots)],
+                send_sem=send_sem.at[1 - side],
+                recv_sem=recv_sem.at[side],
+                device_id={"dom": neighbour, "grp": g},
+                device_id_type=pl.DeviceIdType.MESH,
+            )
+
+            @pl.when(there)
+            def _(copy=copy, back=back):
+                if act == "start":
+                    copy.start()
+                else:
+                    copy.wait_send()
+                    back.wait_recv()
+
+            if act == "start":
+
+                @pl.when(jnp.logical_not(there))
+                def _(side=side):
+                    into[side * slots : (side + 1) * slots, :] = jnp.zeros(
+                        (slots, into.shape[1]), BF
+                    )
+
 
     fill_rows(oh_r, recv_ref, rows, width)
     fill_rows(oh_s, send_ref, rows + 2 * slots, width)
@@ -147,22 +169,23 @@
     fill_columns(oh_st, send_ref, rows + 2 * slots, width)
     fill_columns(oh_xt, rows_ref, rows, width)
 
+    count_copy.wait()
     live = (
-        lax.broadcasted_iota(jnp.int32, (edge_rows, width), 0) < count_ref[0, 0] * width
+        lax.broadcasted_iota(jnp.int32, (edge_rows, width), 0) < count_here[0, 0] * width
     ).astype(F32)
     edges = edges_ref[...]
     at_recv = dot(oh_r[...], nodes).astype(BF)
     at_own = dot(oh_s[:, :rows], nodes)
     first = dot(edges, ew1[:width, :]) + dot(at_recv, ew1[2 * width :, :])
 
-    for copy in halo_copies:
-        copy.wait()
-    from_lower = halo_in[:slots, :] * (d > 0).astype(BF)
-    from_upper = halo_in[slots:, :] * (d < n_dom - 1).astype(BF)
-    at_halo = dot(oh_s[:, rows : rows + slots], from_lower) + dot(
-        oh_s[:, rows + slots :], from_upper
-    )
-    at_send = (at_own + at_halo).astype(BF)
+    part_first[...] = first
+    part_send[...] = at_own
+
+    pl.semaphore_wait(barrier, total - 1)
+    swap(halo_out, halo_in, halo_send, halo_recv, "start")
+    swap(halo_out, halo_in, halo_send, halo_recv, "wait")
+    at_send = (part_send[...] + dot(oh_s[:, rows:], halo_in[...])).astype(BF)
+    first = part_first[...]
     first = first + dot(at_send, ew1[width : 2 * width, :]) + eb1[...]
     sigmoid = lax.logistic(first)
     hidden = (first * sigmoid).astype(BF)
@@ -226,7 +249,7 @@
     high, low = split(at_table[rows:, :])
     w_send = ew1[width : 2 * width, :]
     back_out[...] = (dot_t(high, w_send) + dot_t(low, w_send)).astype(BF)
-    back_copies = swap(back_out, back_in, back_send, back_recv)
+    swap(back_out, back_in, back_send, back_recv, "start")
 
     part_b[:width, :] = row_product(edges, g1_low).astype(BF)
     part_b[width : 2 * width, :] = row_product(at_send, g1_low).astype(BF)
@@ -280,11 +303,8 @@
 
     reduce(part_a, got_a, red_a, all_a, 0)
 
-    for copy in back_copies:
-        copy.wait()
-    back_lower = back_in[:slots, :] * (d > 0).astype(BF)
-    back_upper = back_in[slots:, :] * (d < n_dom - 1).astype(BF)
-    returned = dot(oh_xt[:, :slots], back_lower) + dot(oh_xt[:, slots:], back_upper)
+    swap(back_out, back_in, back_send, back_recv, "wait")
+    returned = dot(oh_xt[...], back_in[...])
     grad_node[...] = (local + returned).astype(BF)
 
     reduce(part_b, got_b, red_b, all_b, 1)
@@ -308,6 +328,16 @@
     drain(got_b, rs_send.at[1])
     drain(all_a, ag_send.at[0])
     drain(all_b, ag_send.at[1])
+
+
+def put_out(*refs):
+    copies = [
+        pltpu.make_async_copy(refs[i], refs[5 + i], refs[10].at[i]) for i in range(5)
+    ]
+    for copy in copies:
+        copy.start()
+    for copy in copies:
+        copy.wait()
 
 
 def shards(
@@ -329,16 +359,17 @@
     grads = 2 * (4 + width) * width + (3 + 2) * width * width
     sem = pltpu.SemaphoreType.DMA((2,))
     table = rows + 2 * slots
-    node_out, edge_out, grad_node, grad_edge, weights = pl.pallas_call(
+    results = (
+        jax.ShapeDtypeStruct((rows, width), BF),
+        jax.ShapeDtypeStruct((edge_rows, width), BF),
+        jax.ShapeDtypeStruct((rows, width), BF),
+        jax.ShapeDtypeStruct((edge_rows, width), BF),
+        jax.ShapeDtypeStruct((grads // width, width), F32),
+    )
+    held = pl.pallas_call(
         functools.partial(kernel, (n_dom, n_grp, chunk, scale)),
-        out_shape=(
-            jax.ShapeDtypeStruct((rows, width), BF),
-            jax.ShapeDtypeStruct((edge_rows, width), BF),
-            jax.ShapeDtypeStruct((rows, width), BF),
-            jax.ShapeDtypeStruct((edge_rows, width), BF),
-            jax.ShapeDtypeStruct((grads // width, width), F32),
-        ),
-        in_specs=[pl.BlockSpec(memory_space=pltpu.SMEM)] + [vmem] * 19,
+        out_shape=tuple(pltpu.VMEM(v.shape, v.dtype) for v in results),
+        in_specs=[pl.BlockSpec(memory_space=pltpu.HBM)] + [vmem] * 19,
         out_specs=[vmem] * 5,
         scratch_shapes=[
             pltpu.VMEM((edge_rows, table), BF),
@@ -348,6 +379,8 @@
             pltpu.VMEM((2 * slots, rows), BF),
             pltpu.VMEM((rows, 2 * slots), BF),
         ]
+        + [pltpu.SMEM((1, 1), jnp.int32), pltpu.SemaphoreType.DMA]
+        + [pltpu.VMEM((edge_rows, width), F32)] * 2
         + [pltpu.VMEM((2 * slots, width), BF)] * 4
         + [pltpu.VMEM((padded, width), BF)] * 4
         + [pltpu.VMEM((chunk, width), BF)] * 2
@@ -366,6 +399,13 @@
         edge_w1, line(edge_b1), edge_w2, line(edge_b2), line(edge_gain), line(edge_shift),
         node_w1, line(node_b1), node_w2, line(node_b2), line(node_gain), line(node_shift),
     )
+    node_out, edge_out, grad_node, grad_edge, weights = pl.pallas_call(
+        put_out,
+        out_shape=results,
+        in_specs=[vmem] * 5,
+        out_specs=[pl.BlockSpec(memory_space=pl.ANY)] * 5,
+        scratch_shapes=[pltpu.SemaphoreType.DMA((5,))],
+    )(*(pltpu.with_memory_space_constraint(v, pltpu.VMEM) for v in held))
     return (
         node_out[None],
         edge_out.reshape(edges.shape),

time: 37.4 us -> 31.7 us (0.85)
  local copies, waits for them, and re-layouts: 5.61 us -> 0 us
    unnamed x11 -> x0, local copies, waits for them, and re-layouts: 5.61 us -> none
    pallas_call x1, Pallas kernels: 30.3 us -> 29.2 us  [shards(): pl.pallas_call(functools.partial(kernel, (n_dom, n_grp, chunk, scale)), o...]
    pallas_call x0 -> x1, Pallas kernels: none -> 0.99 us  [shards(): pl.pallas_call(put_out, out_shape=results, in_specs=[vmem] * 5, out_specs...]
where the time goes in v2:
time: 31.7 us; the launch traced here: 31.5 us
  Pallas kernels  30.2 us (95%)
  between operations  1.29 us (4%)
    pallas_call x1, Pallas kernels, shards(): pl.pallas_call(functools.partial(kernel, (n_dom, n_grp, chunk, scale)), o...  29.2 us
    pallas_call x1, Pallas kernels, shards(): pl.pallas_call(put_out, out_shape=results, in_specs=[vmem] * 5, out_specs...  0.99 us

profile of v2, /device:TPU:0, one launch (start us, length us, event | category | flops | bytes accessed | tf_op | source)
XLA Modules:
  0.0 31.5 jit_solution(9425030311631867714)
XLA Ops:
  1.3 29.2 %shard_map.227 = (bf16[512,128]{1,0:T(8,128)(2,1)S(1)}, bf16[512,128]{1,0:T(8,128)(2,1)S(1)}, bf16[512,128]{1,0:T(8,128)(2,1)S(1)}, bf16[512,128]{1,0:T(8,128)(2,1)S(1)}, f32[904,128]{1,0:T(8,128)S(1)}) custom-call(s32[1,1]{1,0:T(1,128)S(6)} %copy.25.count_ref, bf16[512,128]{1,0:T(8,128)(2,1)} %bitcast.20, bf16[512,128]{1,0:T(8,128)(2,1)} %bitcast.21, ...), custom_call_target="tpu_custom_call" | custom-call | tf_op jit(solution)/shard_map/pallas_call | solution.py:369
  30.5 1.0 %shard_map.228 = (bf16[512,128]{1,0:T(8,128)(2,1)}, bf16[512,128]{1,0:T(8,128)(2,1)}, bf16[512,128]{1,0:T(8,128)(2,1)}, bf16[512,128]{1,0:T(8,128)(2,1)}, f32[904,128]{1,0:T(8,128)}) custom-call(bf16[512,128]{1,0:T(8,128)(2,1)S(1)} %get-tuple-element.15.refs_0_, bf16[512,128]{1,0:T(8,128)(2,1)S(1)} %get-tuple-element.16.refs_1_, ...), custom_call_target="tpu_custom_call" | custom-call | tf_op jit(solution)/shard_map/pallas_call | solution.py:402

commit v3 on v2

--- a/solution.py
+++ b/solution.py
@@ -83,17 +83,32 @@
 
 
 def kernel(
-    sizes,
-    count_ref, nodes_ref, edges_ref, send_ref, recv_ref, rows_ref, ncot_ref, ecot_ref,
-    ew1, eb1, ew2, eb2, eg, es, nw1, nb1, nw2, nb2, ng, ns,
-    node_out, edge_out, grad_node, grad_edge, weight_out,
+    sizes, *refs
+):
+    body(sizes, refs[:20], *refs[20:])
+
+
+def body(
+    sizes, operands, node_out, edge_out, grad_node, grad_edge, weight_out,
     oh_s, oh_st, oh_r, oh_rt, oh_x, oh_xt,
-    count_here, count_sem, part_first, part_send, halo_out, halo_in, back_out, back_in,
+    held, load_sems, part_first, part_send, halo_out, halo_in, back_out, back_in,
     part_a, part_b, got_a, got_b, red_a, red_b, all_a, all_b,
     halo_send, halo_recv, back_send, back_recv,
     rs_send, rs_recv, ag_send, ag_recv,
 ):
     n_dom, n_grp, chunk, scale = sizes
+    (
+        count_here, nodes_ref, edges_ref, send_ref, recv_ref, rows_ref, ncot_ref, ecot_ref,
+        ew1, eb1, ew2, eb2, eg, es, nw1, nb1, nw2, nb2, ng, ns,
+    ) = held
+    loads = [
+        pltpu.make_async_copy(operand, ref, load_sems.at[i])
+        for i, (operand, ref) in enumerate(zip(operands, held))
+    ]
+    early = (5, 1)
+    late = [i for i in range(len(loads)) if i not in early]
+    for i in early:
+        loads[i].start()
     total = n_dom * n_grp
     d = lax.axis_index("dom")
     g = lax.axis_index("grp")
@@ -108,8 +123,6 @@
         t = lax.rem(rank + k, total)
         return t, {"dom": t // n_grp, "grp": lax.rem(t, n_grp)}
 
-    count_copy = pltpu.make_async_copy(count_ref, count_here, count_sem)
-    count_copy.start()
     barrier = pltpu.get_barrier_semaphore()
 
     def greet(k, carry):
@@ -119,6 +132,10 @@
         return carry
 
     lax.fori_loop(1, total, greet, 0)
+    for i in late:
+        loads[i].start()
+    for i in early:
+        loads[i].wait()
 
     nodes = nodes_ref[...]
     fill_rows(oh_x, rows_ref, rows, width)
@@ -163,13 +180,14 @@
                     )
 
 
+    for i in late:
+        loads[i].wait()
     fill_rows(oh_r, recv_ref, rows, width)
     fill_rows(oh_s, send_ref, rows + 2 * slots, width)
     fill_columns(oh_rt, recv_ref, rows, width)
     fill_columns(oh_st, send_ref, rows + 2 * slots, width)
     fill_columns(oh_xt, rows_ref, rows, width)
 
-    count_copy.wait()
     live = (
         lax.broadcasted_iota(jnp.int32, (edge_rows, width), 0) < count_here[0, 0] * width
     ).astype(F32)
@@ -359,35 +377,7 @@
     grads = 2 * (4 + width) * width + (3 + 2) * width * width
     sem = pltpu.SemaphoreType.DMA((2,))
     table = rows + 2 * slots
-    results = (
-        jax.ShapeDtypeStruct((rows, width), BF),
-        jax.ShapeDtypeStruct((edge_rows, width), BF),
-        jax.ShapeDtypeStruct((rows, width), BF),
-        jax.ShapeDtypeStruct((edge_rows, width), BF),
-        jax.ShapeDtypeStruct((grads // width, width), F32),
-    )
-    held = pl.pallas_call(
-        functools.partial(kernel, (n_dom, n_grp, chunk, scale)),
-        out_shape=tuple(pltpu.VMEM(v.shape, v.dtype) for v in results),
-        in_specs=[pl.BlockSpec(memory_space=pltpu.HBM)] + [vmem] * 19,
-        out_specs=[vmem] * 5,
-        scratch_shapes=[
-            pltpu.VMEM((edge_rows, table), BF),
-            pltpu.VMEM((table, edge_rows), BF),
-            pltpu.VMEM((edge_rows, rows), BF),
-            pltpu.VMEM((rows, edge_rows), BF),
-            pltpu.VMEM((2 * slots, rows), BF),
-            pltpu.VMEM((rows, 2 * slots), BF),
-        ]
-        + [pltpu.SMEM((1, 1), jnp.int32), pltpu.SemaphoreType.DMA]
-        + [pltpu.VMEM((edge_rows, width), F32)] * 2
-        + [pltpu.VMEM((2 * slots, width), BF)] * 4
-        + [pltpu.VMEM((padded, width), BF)] * 4
-        + [pltpu.VMEM((chunk, width), BF)] * 2
-        + [pltpu.VMEM((padded, width), BF)] * 2
-        + [sem] * 8,
-        compiler_params=pltpu.CompilerParams(collective_id=0, has_side_effects=True),
-    )(
+    operands = (
         block_count,
         nodes[0],
         edges.reshape(edge_rows, width),
@@ -399,6 +389,36 @@
         edge_w1, line(edge_b1), edge_w2, line(edge_b2), line(edge_gain), line(edge_shift),
         node_w1, line(node_b1), node_w2, line(node_b2), line(node_gain), line(node_shift),
     )
+    results = (
+        jax.ShapeDtypeStruct((rows, width), BF),
+        jax.ShapeDtypeStruct((edge_rows, width), BF),
+        jax.ShapeDtypeStruct((rows, width), BF),
+        jax.ShapeDtypeStruct((edge_rows, width), BF),
+        jax.ShapeDtypeStruct((grads // width, width), F32),
+    )
+    held = pl.pallas_call(
+        functools.partial(kernel, (n_dom, n_grp, chunk, scale)),
+        out_shape=tuple(pltpu.VMEM(v.shape, v.dtype) for v in results),
+        in_specs=[pl.BlockSpec(memory_space=pltpu.HBM)] * len(operands),
+        out_specs=[vmem] * 5,
+        scratch_shapes=[
+            pltpu.VMEM((edge_rows, table), BF),
+            pltpu.VMEM((table, edge_rows), BF),
+            pltpu.VMEM((edge_rows, rows), BF),
+            pltpu.VMEM((rows, edge_rows), BF),
+            pltpu.VMEM((2 * slots, rows), BF),
+            pltpu.VMEM((rows, 2 * slots), BF),
+        ]
+        + [[pltpu.SMEM((1, 1), jnp.int32)] + [pltpu.VMEM(v.shape, v.dtype) for v in operands[1:]]]
+        + [pltpu.SemaphoreType.DMA((len(operands),))]
+        + [pltpu.VMEM((edge_rows, width), F32)] * 2
+        + [pltpu.VMEM((2 * slots, width), BF)] * 4
+        + [pltpu.VMEM((padded, width), BF)] * 4
+        + [pltpu.VMEM((chunk, width), BF)] * 2
+        + [pltpu.VMEM((padded, width), BF)] * 2
+        + [sem] * 8,
+        compiler_params=pltpu.CompilerParams(collective_id=0, has_side_effects=True),
+    )(*operands)
     node_out, edge_out, grad_node, grad_edge, weights = pl.pallas_call(
         put_out,
         out_shape=results,

time: 31.7 us -> 29.1 us (0.918)
  Pallas kernels: 30.2 us -> 27.7 us
    pallas_call x1, Pallas kernels: 29.2 us -> 26.7 us  [shards(): pl.pallas_call(functools.partial(kernel, (n_dom, n_grp, chunk, scale)), o...]
where the time goes in v3:
time: 29.1 us; the launch traced here: 29 us
  Pallas kernels  27.7 us (95%)
  between operations  1.29 us (4%)
    pallas_call x1, Pallas kernels, shards(): pl.pallas_call(functools.partial(kernel, (n_dom, n_grp, chunk, scale)), o...  26.7 us
    pallas_call x1, Pallas kernels, shards(): pl.pallas_call(put_out, out_shape=results, in_specs=[vmem] * 5, out_specs...  0.99 us

profile of v3, /device:TPU:0, one launch (start us, length us, event | category | flops | bytes accessed | tf_op | source)
XLA Modules:
  0.0 29.0 jit_solution(1148664813811942031)
XLA Ops:
  1.3 26.7 %shard_map.227 = (bf16[512,128]{1,0:T(8,128)(2,1)S(1)}, bf16[512,128]{1,0:T(8,128)(2,1)S(1)}, bf16[512,128]{1,0:T(8,128)(2,1)S(1)}, bf16[512,128]{1,0:T(8,128)(2,1)S(1)}, f32[904,128]{1,0:T(8,128)S(1)}) custom-call(s32[1,1]{1,0:T(1,128)S(6)} %copy.25.refs_0_, bf16[512,128]{1,0:T(8,128)(2,1)} %bitcast.20, bf16[512,128]{1,0:T(8,128)(2,1)} %bitcast.21, ...), custom_call_target="tpu_custom_call" | custom-call | tf_op jit(solution)/shard_map/pallas_call | solution.py:399
  28.0 1.0 %shard_map.228 = (bf16[512,128]{1,0:T(8,128)(2,1)}, bf16[512,128]{1,0:T(8,128)(2,1)}, bf16[512,128]{1,0:T(8,128)(2,1)}, bf16[512,128]{1,0:T(8,128)(2,1)}, f32[904,128]{1,0:T(8,128)}) custom-call(bf16[512,128]{1,0:T(8,128)(2,1)S(1)} %get-tuple-element.15.refs_0_, bf16[512,128]{1,0:T(8,128)(2,1)S(1)} %get-tuple-element.16.refs_1_, ...), custom_call_target="tpu_custom_call" | custom-call | tf_op jit(solution)/shard_map/pallas_call | solution.py:422
